TPU v7x, 32 devices: a whole 2x2x4 slice. The times are simulated.
32 devices in a mesh: tm: 16 (over z, y, x), ffn: 2 (over core).
Axes of the slice: x: 2, y: 2, z: 4, core: 2. Of those that a mesh axis runs over, the one named last changes fastest.
Arguments:
- frames: bfloat16 [32768, 512], P('tm'), may hold values from -60 to 60
- upstream: bfloat16 [32768, 512], P('tm'), may hold values from -6 to 6
- recording: int32 [32768], replicated, may hold values from 0 to 3, never falling along the last dimension, each value on 1 to 16384 neighbouring positions
- first_gain: float32 [512], replicated, may hold values from 0.1 to 1.9
- query_weight: bfloat16 [512, 512], P(None, 'ffn'), may hold values from -0.5 to 0.5
- key_weight: bfloat16 [512, 512], P(None, 'ffn'), may hold values from -0.5 to 0.5
- value_weight: bfloat16 [512, 512], P(None, 'ffn'), may hold values from -0.25 to 0.25
- out_weight: bfloat16 [512, 512], P('ffn'), may hold values from -0.25 to 0.25
- second_gain: float32 [512], replicated, may hold values from 0.1 to 1.9
- inner_weight: bfloat16 [512, 2048], P(None, 'ffn'), may hold values from -0.25 to 0.25
- outer_weight: bfloat16 [2048, 512], P('ffn'), may hold values from -0.125 to 0.125
Outputs:
- grad_frames: float32 [32768, 512], P(('tm', 'ffn'))
- grad_query_weight: float32 [512, 512], P(None, 'ffn')
- grad_key_weight: float32 [512, 512], P(None, 'ffn')
- grad_value_weight: float32 [512, 512], P(None, 'ffn')
- grad_out_weight: float32 [512, 512], P('ffn')
- grad_inner_weight: float32 [512, 2048], P(None, 'ffn')
- grad_outer_weight: float32 [2048, 512], P('ffn')
Inputs may be any that keep to these rules, and one draw needn't show every extreme that they name: Ids never fall along time; each recording spans 1 to 16384 frames and one spans exactly that many.
All inputs are finite; a program needn't handle non-finite values.
Results may differ from a plain program's by a relative error of at most 0.025.
Values may be sent and summed in bfloat16 or wider, within the bound.
A program may use at most 128 MiB of HBM per device.

v0:
```python
import math
import jax
import jax.numpy as jnp
from jax import lax
from jax.sharding import PartitionSpec as P

HEAD_DIM = 64
HALF = 256
epsilon = 1e-05
masked_score = -1e30


def with_halo(cells, sides, width):
    for axis, dim in sides:
        count = lax.axis_size(axis)
        ends = count - 1
        head = lax.slice_in_dim(cells, 0, width, axis=dim)
        tail = lax.slice_in_dim(cells, cells.shape[dim] - width, cells.shape[dim], axis=dim)
        cells = jnp.concatenate(
            [
                lax.ppermute(tail, axis, [(i, (i + 1) % count) for i in range(ends)]),
                cells,
                lax.ppermute(head, axis, [((i + 1) % count, i) for i in range(ends)]),
            ],
            axis=dim,
        )
    return cells


def layer_norm(inputs):
    center = jnp.mean(inputs, axis=-1, keepdims=True)
    shifted = inputs - center
    inverse = lax.rsqrt(jnp.mean(shifted * shifted, axis=-1, keepdims=True) + epsilon)
    return (shifted * inverse, inverse)


def norm_back(grad_normed, scaled, inverse, gain):
    weighted = grad_normed * gain
    first_mean = jnp.mean(weighted, axis=-1, keepdims=True)
    second_mean = jnp.mean(weighted * scaled, axis=-1, keepdims=True)
    return inverse * (weighted - first_mean - scaled * second_mean)


def project(normed, weight):
    return jnp.dot(normed, weight, preferred_element_type=jnp.float32).astype(jnp.bfloat16)


def block_allowed(record_query, record_key):
    block_rows = record_query.shape[0]
    offsets = lax.broadcasted_iota(
        jnp.int32, (block_rows, 2 * block_rows), 1
    ) - lax.broadcasted_iota(jnp.int32, (block_rows, 2 * block_rows), 0)
    band = (offsets >= 0) & (offsets < block_rows)
    return band & (record_query[:, None] == record_key[None, :])


def masked_scores(query_block, key_block, allowed):
    scores = jnp.einsum(
        "qhd,khd->hqk", query_block, key_block, preferred_element_type=jnp.float32
    ) * HEAD_DIM ** (-0.5)
    return jnp.where(allowed[None], scores, masked_score)


def tile_scores(query_block, key_block, allowed):
    return masked_scores(query_block, key_block, allowed)


def softmax_rows(scores):
    peak = jnp.max(scores, axis=-1, keepdims=True)
    weights = jnp.exp(scores - peak)
    return weights / jnp.sum(weights, axis=-1, keepdims=True)


def score_grads(grad_block, value_tile):
    return jnp.einsum("qhd,khd->hqk", grad_block, value_tile, preferred_element_type=jnp.float32)


def query_grads(score_tile, key_tile):
    return jnp.einsum("hqk,khd->qhd", score_tile, key_tile, preferred_element_type=jnp.float32)


def key_grads(score_tile, query_block):
    return jnp.einsum("hqk,qhd->khd", score_tile, query_block, preferred_element_type=jnp.float32)


def block_context(query_block, key_block, value_block, allowed):
    probability = softmax_rows(tile_scores(query_block, key_block, allowed))
    context = jnp.einsum(
        "hqk,khd->qhd",
        probability.astype(jnp.bfloat16),
        value_block,
        preferred_element_type=jnp.float32,
    )
    return context.astype(jnp.bfloat16)


def block_backward(query_block, key_block, value_block, grad_block, allowed):
    probability = softmax_rows(tile_scores(query_block, key_block, allowed))
    probability_low = probability.astype(jnp.bfloat16)
    grad_prob = score_grads(grad_block, value_block)
    inner_sum = jnp.sum(grad_prob * probability, axis=-1, keepdims=True)
    grad_scores = (probability * (grad_prob - inner_sum) * HEAD_DIM ** (-0.5)).astype(jnp.bfloat16)
    grad_query = query_grads(grad_scores, key_block)
    grad_key = key_grads(grad_scores, query_block)
    grad_value = key_grads(probability_low, grad_block)
    return (grad_query, grad_key, grad_value)


def local(
    frames,
    upstream,
    recording,
    first_gain,
    query_weight,
    key_weight,
    value_weight,
    out_weight,
    second_gain,
    inner_weight,
    outer_weight,
):
    slab_rows = frames.shape[0]
    block_rows = 2 * HALF
    head_cols = query_weight.shape[1]
    local_heads = head_cols // HEAD_DIM
    share_rows = slab_rows // lax.axis_size("ffn")
    share_start = lax.axis_index("ffn") * share_rows
    record_pad = jnp.pad(recording, (HALF, HALF), constant_values=-1)
    record_ext = lax.dynamic_slice_in_dim(
        record_pad, lax.axis_index("tm") * slab_rows, slab_rows + 2 * HALF
    )
    frames_wide = frames.astype(jnp.float32)
    upstream_wide = upstream.astype(jnp.float32)
    scaled_first, inverse_first = layer_norm(frames_wide)
    normed_first = (scaled_first * first_gain).astype(jnp.bfloat16)
    queries = project(normed_first, query_weight)
    key_rows = project(normed_first, key_weight)
    value_rows = project(normed_first, value_weight)
    key_value = jnp.concatenate([key_rows, value_rows], axis=1)
    key_value_ext = with_halo(key_value, (("tm", 0),), HALF)
    blocks = slab_rows // block_rows
    pieces = []
    contexts = []
    for block_index in range(blocks):
        first_row = block_index * block_rows
        query_block = queries[first_row : first_row + block_rows].reshape(
            block_rows, local_heads, HEAD_DIM
        )
        ext_block = key_value_ext[first_row : first_row + 2 * block_rows]
        key_block = ext_block[:, :head_cols].reshape(2 * block_rows, local_heads, HEAD_DIM)
        value_block = ext_block[:, head_cols:].reshape(2 * block_rows, local_heads, HEAD_DIM)
        allowed = block_allowed(
            record_ext[HALF + first_row : HALF + first_row + block_rows],
            record_ext[first_row : first_row + 2 * block_rows],
        )
        pieces.append((query_block, key_block, value_block, allowed))
        contexts.append(
            block_context(query_block, key_block, value_block, allowed).reshape(
                block_rows, head_cols
            )
        )
    context = jnp.concatenate(contexts, axis=0)
    partial_value = jnp.dot(context, out_weight, preferred_element_type=jnp.float32)
    middle = frames_wide + lax.psum(partial_value.astype(jnp.bfloat16), "ffn").astype(jnp.float32)
    scaled_second, inverse_second = layer_norm(middle)
    normed_second = (scaled_second * second_gain).astype(jnp.bfloat16)
    inner_pre = jnp.dot(normed_second, inner_weight, preferred_element_type=jnp.float32)
    activation = jax.nn.silu(inner_pre).astype(jnp.bfloat16)
    sigmoid_inner = jax.nn.sigmoid(inner_pre)
    grad_act = jnp.dot(upstream, outer_weight.T, preferred_element_type=jnp.float32) * 0.5
    grad_inner = (grad_act * sigmoid_inner * (1.0 + inner_pre * (1.0 - sigmoid_inner))).astype(
        jnp.bfloat16
    )
    grad_outer_terms = jnp.dot(activation.T, upstream, preferred_element_type=jnp.float32) * 0.5
    grad_inner_terms = jnp.dot(normed_second.T, grad_inner, preferred_element_type=jnp.float32)
    grad_second_part = jnp.dot(grad_inner, inner_weight.T, preferred_element_type=jnp.float32)
    grad_second = lax.psum(grad_second_part.astype(jnp.bfloat16), "ffn").astype(jnp.float32)
    grad_middle = upstream_wide + norm_back(grad_second, scaled_second, inverse_second, second_gain)
    grad_middle_low = grad_middle.astype(jnp.bfloat16)
    grad_middle_share = lax.dynamic_slice_in_dim(grad_middle, share_start, share_rows, 0)
    grad_out_terms = jnp.dot(context.T, grad_middle_low, preferred_element_type=jnp.float32)
    grad_context = jnp.dot(
        grad_middle_low, out_weight.T, preferred_element_type=jnp.float32
    ).astype(jnp.bfloat16)
    grad_pairs_ext = jnp.zeros((slab_rows + 2 * HALF, 2 * head_cols), jnp.float32)
    query_parts = []
    for block_index, (query_block, key_block, value_block, allowed) in enumerate(pieces):
        first_row = block_index * block_rows
        grad_block = grad_context[first_row : first_row + block_rows].reshape(
            block_rows, local_heads, HEAD_DIM
        )
        grad_query, grad_key, grad_value = block_backward(
            query_block, key_block, value_block, grad_block, allowed
        )
        query_parts.append(grad_query.reshape(block_rows, head_cols))
        grad_pair = jnp.concatenate(
            [
                grad_key.reshape(2 * block_rows, head_cols),
                grad_value.reshape(2 * block_rows, head_cols),
            ],
            axis=1,
        )
        grad_pairs_ext = grad_pairs_ext.at[first_row : first_row + 2 * block_rows].add(grad_pair)
    outer_rims = jnp.concatenate(
        [grad_pairs_ext[:HALF], grad_pairs_ext[slab_rows + HALF :]], axis=0
    )
    received = with_halo(outer_rims.astype(jnp.bfloat16), (("tm", 0),), HALF).astype(
        outer_rims.dtype
    )
    from_lower = received[:HALF]
    from_upper = received[3 * HALF :]
    grad_pairs = grad_pairs_ext[HALF : HALF + slab_rows]
    grad_pairs = (
        grad_pairs
        + jnp.pad(from_lower, ((0, slab_rows - HALF), (0, 0)))
        + jnp.pad(from_upper, ((slab_rows - HALF, 0), (0, 0)))
    )
    grad_query_low = jnp.concatenate(query_parts, axis=0).astype(jnp.bfloat16)
    grad_key_low = grad_pairs[:, :head_cols].astype(jnp.bfloat16)
    grad_value_low = grad_pairs[:, head_cols:].astype(jnp.bfloat16)
    grad_query_terms = jnp.dot(normed_first.T, grad_query_low, preferred_element_type=jnp.float32)
    grad_key_terms = jnp.dot(normed_first.T, grad_key_low, preferred_element_type=jnp.float32)
    grad_value_terms = jnp.dot(normed_first.T, grad_value_low, preferred_element_type=jnp.float32)
    grad_first_part = jnp.dot(grad_query_low, query_weight.T, preferred_element_type=jnp.float32)
    grad_first_part = grad_first_part + jnp.dot(
        grad_key_low, key_weight.T, preferred_element_type=jnp.float32
    )
    grad_first_part = grad_first_part + jnp.dot(
        grad_value_low, value_weight.T, preferred_element_type=jnp.float32
    )
    grad_first_share = lax.psum_scatter(
        grad_first_part.astype(jnp.bfloat16), "ffn", scatter_dimension=0, tiled=True
    ).astype(jnp.float32)
    scaled_share = lax.dynamic_slice_in_dim(scaled_first, share_start, share_rows, 0)
    inverse_share = lax.dynamic_slice_in_dim(inverse_first, share_start, share_rows, 0)
    grad_frames = grad_middle_share + norm_back(
        grad_first_share, scaled_share, inverse_share, first_gain
    )
    weight_scale = 1.0 / math.sqrt(recording.shape[0])
    totals = (
        lax.psum(grad_query_terms.astype(jnp.bfloat16), "tm").astype(jnp.float32),
        lax.psum(grad_key_terms.astype(jnp.bfloat16), "tm").astype(jnp.float32),
        lax.psum(grad_value_terms.astype(jnp.bfloat16), "tm").astype(jnp.float32),
        lax.psum(grad_out_terms.astype(jnp.bfloat16), "tm").astype(jnp.float32),
        lax.psum(grad_inner_terms.astype(jnp.bfloat16), "tm").astype(jnp.float32),
        lax.psum(grad_outer_terms.astype(jnp.bfloat16), "tm").astype(jnp.float32),
    )
    return (grad_frames,) + tuple((total * weight_scale for total in totals))


def solution(mesh):
    in_specs = (
        P("tm", None),
        P("tm", None),
        P(),
        P(),
        P(None, "ffn"),
        P(None, "ffn"),
        P(None, "ffn"),
        P("ffn", None),
        P(),
        P(None, "ffn"),
        P("ffn", None),
    )
    out_specs = (
        P(("tm", "ffn"), None),
        P(None, "ffn"),
        P(None, "ffn"),
        P(None, "ffn"),
        P("ffn", None),
        P(None, "ffn"),
        P("ffn", None),
    )
    return jax.shard_map(local, mesh=mesh, in_specs=in_specs, out_specs=out_specs, check_vma=False)
```

profile of v0, /device:TPU:0, one launch (start us, length us, event | category | flops | bytes accessed | tf_op | source)
XLA Modules:
  0.0 560.0 jit_solution(10052441508470068500)
XLA Ops:
  7.3 2.1 convert_reduce_fusion
  9.4 2.5 fusion.26
  11.9 2.4 fusion.24
  16.8 5.6 collective-permute-start
  24.1 1.6 compare_and_fusion.2
  25.7 1.7 compare_and_fusion
  27.4 2.3 convolution_convert_fusion.3
  30.6 2.5 collective-permute-done
  33.2 1.9 collective-permute-done.1
  35.1 3.2 pad_maximum_fusion.5
  38.3 7.5 %fusion.168 = (f32[4,512]{1,0:T(4,128)S(1)}, f32[4,512,1024]{2,1,0:T(8,128)}) fusion(pred[512,1024]{1,0:T(8,128)(4,1)} %get-tuple-element.110, bf16[512,4,64]{0,2,1:T(8,128)(2,1)} %bitcast.159, bf16[1024,4,64]{0,2,1:T(8,128)(2,1)} %bitcast.151), kind=kOutput, calls=%fused_computation.222 | convolution fusion | flops 276825088 | bytes 9707520 | tf_op jit(solution)/shard_map/sub | solution.py:70
  45.7 5.7 %fusion.92 = bf16[4,64,512]{2,1,0:T(8,128)(2,1)} fusion(bf16[1024,4,64]{0,2,1:T(8,128)(2,1)} %bitcast.127, f32[4,512,1024]{2,1,0:T(8,128)} %get-tuple-element.106, f32[4,512]{1,0:T(4,128)S(1)} %get-tuple-element.105), kind=kOutput, calls=%fused_computation.125 | convolution fusion | flops 272760832 | bytes 9183232 | tf_op jit(solution)/shard_map/hqk,khd->qhd/dot_general | solution.py:88
  51.5 7.4 %fusion.165 = (f32[4,512]{1,0:T(4,128)S(1)}, f32[4,512,1024]{2,1,0:T(8,128)}) fusion(pred[512,1024]{1,0:T(8,128)(4,1)} %get-tuple-element.107, bf16[512,4,64]{0,2,1:T(8,128)(2,1)S(1)} %bitcast.157, bf16[1024,4,64]{0,2,1:T(8,128)(2,1)} %bitcast.149), kind=kOutput, calls=%fused_computation.219 | convolution fusion | flops 276825088 | bytes 9707520 | tf_op jit(solution)/shard_map/sub | solution.py:70
  58.9 5.8 %fusion.101 = bf16[4,64,512]{2,1,0:T(8,128)(2,1)} fusion(bf16[1024,4,64]{0,2,1:T(8,128)(2,1)} %bitcast.125, f32[4,512,1024]{2,1,0:T(8,128)} %get-tuple-element.100, f32[4,512]{1,0:T(4,128)S(1)} %get-tuple-element.99), kind=kOutput, calls=%fused_computation.128 | convolution fusion | flops 272760832 | bytes 9183232 | tf_op jit(solution)/shard_map/hqk,khd->qhd/dot_general | solution.py:88
  64.7 7.7 %fusion.166 = (f32[4,512]{1,0:T(4,128)S(1)}, f32[4,512,1024]{2,1,0:T(8,128)}) fusion(pred[512,1024]{1,0:T(8,128)(4,1)} %get-tuple-element.108, bf16[512,4,64]{0,2,1:T(8,128)(2,1)S(1)} %bitcast.161, bf16[1024,4,64]{0,2,1:T(8,128)(2,1)} %bitcast.153), kind=kOutput, calls=%fused_computation.220 | convolution fusion | flops 276825088 | bytes 9707520 | tf_op jit(solution)/shard_map/sub | solution.py:70
  72.4 5.8 %fusion.98 = bf16[4,64,512]{2,1,0:T(8,128)(2,1)} fusion(bf16[1024,4,64]{0,2,1:T(8,128)(2,1)} %bitcast.129, f32[4,512,1024]{2,1,0:T(8,128)} %get-tuple-element.102, f32[4,512]{1,0:T(4,128)S(1)} %get-tuple-element.101), kind=kOutput, calls=%fused_computation.127 | convolution fusion | flops 272760832 | bytes 9183232 | tf_op jit(solution)/shard_map/hqk,khd->qhd/dot_general | solution.py:88
  78.1 7.4 %fusion.167 = (f32[4,512]{1,0:T(4,128)S(1)}, f32[4,512,1024]{2,1,0:T(8,128)}) fusion(pred[512,1024]{1,0:T(8,128)(4,1)} %get-tuple-element.109, bf16[512,4,64]{0,2,1:T(8,128)(2,1)S(1)} %bitcast.163, bf16[1024,4,64]{0,2,1:T(8,128)(2,1)} %bitcast.155), kind=kOutput, calls=%fused_computation.221 | convolution fusion | flops 276825088 | bytes 9707520 | tf_op jit(solution)/shard_map/sub | solution.py:70
  85.6 5.1 fusion.95
  91.4 2.1 convolution_convert_fusion.1
  93.9 21.3 %all-reduce.9.cloned.1.call-done = bf16[2048,512]{1,0:T(8,128)(2,1)} async-done(((bf16[2048,512]{1,0:T(8,128)(2,1)}), bf16[2048,512]{1,0:T(8,128)(2,1)}) %all-reduce.9.cloned.1.call-update) | async-done | bytes 2097168 | tf_op jit(solution)/shard_map/psum | solution.py:164
  115.2 2.4 fusion.68
  118.6 2.8 fusion.162
  121.4 5.3 multiply_convert_fusion.5
  126.7 1.9 copy-done.67
  128.7 3.8 convolution_convert_fusion
  132.5 6.5 %convolution_convert_fusion.6 = bf16[512,1024]{1,0:T(8,128)(2,1)} fusion(bf16[2048,1024]{1,0:T(8,128)(2,1)} %copy-done.67, bf16[2048,512]{1,0:T(8,128)(2,1)} %all-reduce.9.cloned.1.call-done, bf16[2048,512]{1,0:T(8,128)(2,1)S(1)} %copy-done.2, f32[512]{0:T(512)S(1)} %copy-done.55, f32[2048]{0:T(1024)S(1)} %add_rsqrt_fusion, ...), kind=kOutput, calls=%fused_computation.124 | convolution fusion | flops 2155347968 | bytes 9455616 | tf_op jit(solution)/shard_map/dot_general | solution.py:175
  139.0 3.4 multiply_convert_fusion.9
  142.4 12.7 %all-reduce.11.cloned.1.call-done = bf16[2048,512]{1,0:T(8,128)(2,1)} async-done(((bf16[2048,512]{1,0:T(8,128)(2,1)}), bf16[2048,512]{1,0:T(8,128)(2,1)}) %all-reduce.11.cloned.1.call-update) | async-done | bytes 2097168 | tf_op jit(solution)/shard_map/psum | solution.py:177
  155.1 4.0 fusion.29
  159.2 2.3 multiply_add_fusion
  161.6 1.5 convolution_convert_fusion.7
  165.4 1.9 fusion.81
  167.4 4.5 fusion.170
  171.9 22.1 %fusion.110 = bf16[4,64,512]{2,1,0:T(8,128)(2,1)} fusion(bf16[1024,4,64]{0,2,1:T(8,128)(2,1)S(1)} %bitcast.156, f32[4,512,1024]{2,1,0:T(8,128)} %fusion.170, f32[4,512,1024]{2,1,0:T(8,128)} %get-tuple-element.104, f32[4,512]{1,0:T(4,128)S(1)} %get-tuple-element.103), kind=kOutput, calls=%fused_computation.131 | convolution fusion | flops 283249664 | bytes 17571840 | tf_op jit(solution)/shard_map/hqk,khd->qhd/dot_general | solution.py:79
  194.1 18.3 %fusion.50 = f32[4,64,1024]{2,1,0:T(8,128)} fusion(bf16[512,4,64]{0,2,1:T(8,128)(2,1)S(1)} %bitcast.164, f32[4,512,1024]{2,1,0:T(8,128)} %fusion.170, f32[4,512,1024]{2,1,0:T(8,128)} %get-tuple-element.104, f32[4,512]{1,0:T(4,128)S(1)} %get-tuple-element.103), kind=kOutput, calls=%fused_computation.73 | convolution fusion | flops 283118592 | bytes 18096128 | tf_op jit(solution)/shard_map/hqk,qhd->khd/dot_general | solution.py:83
  212.4 5.3 fusion.77
  217.7 4.5 fusion.171
  222.2 21.9 %fusion.107 = bf16[4,64,512]{2,1,0:T(8,128)(2,1)} fusion(bf16[1024,4,64]{0,2,1:T(8,128)(2,1)S(1)} %bitcast.154, f32[4,512,1024]{2,1,0:T(8,128)} %fusion.171, f32[4,512,1024]{2,1,0:T(8,128)} %get-tuple-element.102, f32[4,512]{1,0:T(4,128)S(1)} %get-tuple-element.101), kind=kOutput, calls=%fused_computation.130 | convolution fusion | flops 283249664 | bytes 17571840 | tf_op jit(solution)/shard_map/hqk,khd->qhd/dot_general | solution.py:79
  244.2 18.5 %fusion.56 = f32[4,64,1024]{2,1,0:T(8,128)} fusion(bf16[512,4,64]{0,2,1:T(8,128)(2,1)S(1)} %bitcast.162, f32[4,512,1024]{2,1,0:T(8,128)} %fusion.171, f32[4,512,1024]{2,1,0:T(8,128)} %get-tuple-element.102, f32[4,512]{1,0:T(4,128)S(1)} %get-tuple-element.101), kind=kOutput, calls=%fused_computation.75 | convolution fusion | flops 283118592 | bytes 18096128 | tf_op jit(solution)/shard_map/hqk,qhd->khd/dot_general | solution.py:83
  262.7 4.4 fusion.85
  267.1 4.6 fusion.169
  271.7 21.9 %fusion.113 = bf16[4,64,512]{2,1,0:T(8,128)(2,1)} fusion(bf16[1024,4,64]{0,2,1:T(8,128)(2,1)S(1)} %bitcast.152, f32[4,512,1024]{2,1,0:T(8,128)} %fusion.169, f32[4,512,1024]{2,1,0:T(8,128)} %get-tuple-element.106, f32[4,512]{1,0:T(4,128)S(1)} %copy-done.71), kind=kOutput, calls=%fused_computation.132 | convolution fusion | flops 283249664 | bytes 17571840 | tf_op jit(solution)/shard_map/hqk,khd->qhd/dot_general | solution.py:79
  293.6 18.3 %fusion.44 = f32[4,64,1024]{2,1,0:T(8,128)} fusion(bf16[512,4,64]{0,2,1:T(8,128)(2,1)S(1)} %bitcast.160, f32[4,512,1024]{2,1,0:T(8,128)} %fusion.169, f32[4,512,1024]{2,1,0:T(8,128)} %get-tuple-element.106, f32[4,512]{1,0:T(4,128)S(1)} %copy-done.71), kind=kOutput, calls=%fused_computation.71 | convolution fusion | flops 283118592 | bytes 18096128 | tf_op jit(solution)/shard_map/hqk,qhd->khd/dot_general | solution.py:83
  311.9 4.4 fusion.73
  316.3 4.5 fusion.172
  320.8 21.9 %fusion.104 = bf16[4,64,512]{2,1,0:T(8,128)(2,1)} fusion(bf16[1024,4,64]{0,2,1:T(8,128)(2,1)S(1)} %bitcast.150, f32[4,512,1024]{2,1,0:T(8,128)} %fusion.172, f32[4,512,1024]{2,1,0:T(8,128)} %get-tuple-element.100, f32[4,512]{1,0:T(4,128)S(1)} %copy-done.69), kind=kOutput, calls=%fused_computation.129 | convolution fusion | flops 283249664 | bytes 17571840 | tf_op jit(solution)/shard_map/hqk,khd->qhd/dot_general | solution.py:79
  342.7 18.6 %fusion.62 = f32[4,64,1024]{2,1,0:T(8,128)} fusion(bf16[512,4,64]{0,2,1:T(8,128)(2,1)S(1)} %bitcast.158, f32[4,512,1024]{2,1,0:T(8,128)} %fusion.172, f32[4,512,1024]{2,1,0:T(8,128)} %get-tuple-element.100, f32[4,512]{1,0:T(4,128)S(1)} %copy-done.69), kind=kOutput, calls=%fused_computation.77 | convolution fusion | flops 283118592 | bytes 18096128 | tf_op jit(solution)/shard_map/hqk,qhd->khd/dot_general | solution.py:83
  367.0 4.6 collective-permute-start.2
  371.6 1.5 convolution_convert_fusion.10
  373.1 3.7 collective-permute-done.3
  376.8 6.0 %collective-permute-done.2 = bf16[256,512]{0,1:T(8,128)(2,1)S(1)} collective-permute-done((bf16[256,512]{0,1:T(8,128)(2,1)S(1)}, bf16[256,512]{0,1:T(8,128)(2,1)S(1)}, u32[]{:S(2)}, u32[]{:S(2)}) %collective-permute-start.2) | collective-permute-done | bytes 262176 | tf_op jit(solution)/shard_map/ppermute | solution.py:21
  383.3 1.5 convolution_convert_fusion.9
  384.8 1.5 convolution_convert_fusion.8
  386.4 1.7 fusion.132
  389.0 2.1 add_convert_fusion
  391.2 143.1 %all-reduce.13.cloned.1.call-done = (bf16[512,256]{1,0:T(8,128)(2,1)}, bf16[512,256]{1,0:T(8,128)(2,1)}, bf16[512,256]{1,0:T(8,128)(2,1)}, bf16[256,512]{1,0:T(8...) async-done(((bf16[512,256]{1,0:T(8,128)(2,1)}, bf16[512,256]{1,0:T(8,128)(2,1)}, bf16[512,256]{1,0:T(8,128)(2,1)}, bf16[256,512]{1,0:T(8,128)(2,1)}, ...) | async-done | bytes 3145744 | tf_op jit(solution)/shard_map/psum | solution.py:241
  534.3 1.9 convert_multiply_fusion.7
  536.2 1.8 convert_multiply_fusion.6
  538.0 1.8 convert_multiply_fusion.5
  539.8 1.8 convert_multiply_fusion.4
  541.6 2.9 convert_multiply_fusion.2
  544.5 1.6 convert_multiply_fusion.1
  546.1 2.4 fusion.72
  548.6 4.4 multiply_add_fusion.1
  (187 shorter events, 17.0 us)
Async XLA Ops:
  7.2 111.4 %copy-start = (bf16[512,1024]{1,0:T(8,128)(2,1)S(1)}, bf16[512,1024]{1,0:T(8,128)(2,1)}, u32[]{:S(2)}) copy-start(bf16[512,1024]{1,0:T(8,128)(2,1)} %param.28) | copy-start | bytes 3145732
  7.2 4.7 copy-start.2
  7.2 4.7 copy-start.53
  7.2 108.0 %all-reduce.9.cloned.1.call-start = ((), (), s32[]{:S(2)}) async-start(), calls=%async_computation.1 | async-start | bytes 4194304 | tf_op jit(solution)/shard_map/psum | solution.py:164
  11.9 2.4 copy-start.52
  11.9 2.4 copy-start.29
  11.9 3.2 copy-start.27
  14.3 2.5 copy-start.3
  14.3 9.5 %copy-start.37 = (s32[32768]{0:T(1024)S(1)}, s32[32768]{0:T(1024)}, u32[]{:S(2)}) copy-start(s32[32768]{0:T(1024)} %param.21) | copy-start | bytes 393220
  15.1 12.3 %copy-start.31 = (bf16[512,256]{1,0:T(8,128)(2,1)S(1)}, bf16[512,256]{1,0:T(8,128)(2,1)}, u32[]{:S(2)}) copy-start(bf16[512,256]{1,0:T(8,128)(2,1)} %param.23) | copy-start | bytes 786436
  15.9 6.5 %copy-start.10 = (bf16[2048,256]{0,1:T(8,128)(2,1)}, bf16[2048,256]{0,1:T(8,128)(2,1)S(1)}, u32[]{:S(2)}) copy-start(bf16[2048,256]{0,1:T(8,128)(2,1)S(1)} %convolution_convert_fusion.5) | copy-start | bytes 3145732
  16.8 16.4 %collective-permute-start = (bf16[256,512]{0,1:T(8,128)(2,1)}, bf16[256,512]{0,1:T(8,128)(2,1)}, u32[]{:S(2)}, u32[]{:S(2)}) collective-permute-start(bf16[256,512]{0,1:T(8,128)(2,1)} %get-tuple-element.75), channel_id=1, source_target_pairs={{0,2},{2,4},{4,6},{6,8},{8,10},{10,12},{12,14},{14,16},{16,18},{18... | collective-permute-start | bytes 786440 | tf_op jit(solution)/shard_map/ppermute | solution.py:21
  22.4 12.7 %collective-permute-start.1 = (bf16[256,512]{0,1:T(8,128)(2,1)}, bf16[256,512]{0,1:T(8,128)(2,1)}, u32[]{:S(2)}, u32[]{:S(2)}) collective-permute-start(bf16[256,512]{0,1:T(8,128)(2,1)} %get-tuple-element.76), channel_id=1, source_target_pairs={{2,0},{4,2},{6,4},{8,6},{10,8},{12,10},{14,12},{16,14},{18,16},{20... | collective-permute-start | bytes 786440 | tf_op jit(solution)/shard_map/ppermute | solution.py:23
  23.8 11.2 %copy-start.9 = (bf16[2048,256]{0,1:T(8,128)(2,1)S(1)}, bf16[2048,256]{0,1:T(8,128)(2,1)}, u32[]{:S(2)}) copy-start(bf16[2048,256]{0,1:T(8,128)(2,1)} %copy-done.8) | copy-start | bytes 3145732
  23.8 11.2 %copy-start.11 = (bf16[2048,256]{0,1:T(8,128)(2,1)S(1)}, bf16[2048,256]{0,1:T(8,128)(2,1)}, u32[]{:S(2)}) copy-start(bf16[2048,256]{0,1:T(8,128)(2,1)} %copy-done.10) | copy-start | bytes 3145732
  30.6 20.9 %copy-start.38 = (bf16[512,256]{0,1:T(8,128)(2,1)}, bf16[512,256]{0,1:T(8,128)(2,1)S(1)}, u32[]{:S(2)}) copy-start(bf16[512,256]{0,1:T(8,128)(2,1)S(1)} %get-tuple-element.88) | copy-start | bytes 786436
  45.7 5.7 %copy-start.70 = (f32[4,512]{1,0:T(4,128)}, f32[4,512]{1,0:T(4,128)S(1)}, u32[]{:S(2)}) copy-start(f32[4,512]{1,0:T(4,128)S(1)} %get-tuple-element.105) | copy-start | bytes 24580
  58.9 5.8 %copy-start.68 = (f32[4,512]{1,0:T(4,128)}, f32[4,512]{1,0:T(4,128)S(1)}, u32[]{:S(2)}) copy-start(f32[4,512]{1,0:T(4,128)S(1)} %get-tuple-element.99) | copy-start | bytes 24580
  58.9 5.8 %copy-start.41 = (bf16[512,256]{0,1:T(8,128)(2,1)S(1)}, bf16[512,256]{0,1:T(8,128)(2,1)}, u32[]{:S(2)}) copy-start(bf16[512,256]{0,1:T(8,128)(2,1)} %get-tuple-element.89) | copy-start | bytes 786436
  72.4 5.8 %copy-start.43 = (bf16[512,256]{0,1:T(8,128)(2,1)S(1)}, bf16[512,256]{0,1:T(8,128)(2,1)}, u32[]{:S(2)}) copy-start(bf16[512,256]{0,1:T(8,128)(2,1)} %get-tuple-element.90) | copy-start | bytes 786436
  85.6 5.8 %copy-start.45 = (bf16[256,512]{1,0:T(8,128)(2,1)S(1)}, bf16[256,512]{1,0:T(8,128)(2,1)}, u32[]{:S(2)}) copy-start(bf16[256,512]{1,0:T(8,128)(2,1)} %param.26) | copy-start | bytes 786436
  85.6 5.8 %copy-start.57 = (bf16[4,64,512]{2,1,0:T(8,128)(2,1)S(1)}, bf16[4,64,512]{2,1,0:T(8,128)(2,1)}, u32[]{:S(2)}) copy-start(bf16[4,64,512]{2,1,0:T(8,128)(2,1)} %fusion.92) | copy-start | bytes 786436
  85.6 5.8 %copy-start.59 = (bf16[4,64,512]{2,1,0:T(8,128)(2,1)S(1)}, bf16[4,64,512]{2,1,0:T(8,128)(2,1)}, u32[]{:S(2)}) copy-start(bf16[4,64,512]{2,1,0:T(8,128)(2,1)} %fusion.101) | copy-start | bytes 786436
  85.6 5.8 %copy-start.61 = (bf16[4,64,512]{2,1,0:T(8,128)(2,1)S(1)}, bf16[4,64,512]{2,1,0:T(8,128)(2,1)}, u32[]{:S(2)}) copy-start(bf16[4,64,512]{2,1,0:T(8,128)(2,1)} %fusion.98) | copy-start | bytes 786436
  93.5 25.1 %copy-start.55 = (f32[512]{0:T(512)S(1)}, f32[512]{0:T(512)}, u32[]{:S(2)}) copy-start(f32[512]{0:T(512)} %param.27) | copy-start | bytes 6148
  93.5 61.6 %all-reduce.11.cloned.1.call-start = ((), (), s32[]{:S(2)}) async-start(), calls=%async_computation.2 | async-start | bytes 4194304 | tf_op jit(solution)/shard_map/psum | solution.py:177
  118.6 2.8 copy-start.17
  118.6 2.8 copy-start.56
  121.4 5.3 copy-start.65
  132.5 401.8 %all-reduce.13.cloned.1.call-start = ((), (), s32[]{:S(2)}) async-start(), calls=%async_computation.4 | async-start | bytes 6291456 | tf_op jit(solution)/shard_map/psum | solution.py:241
  132.5 6.5 %copy-start.18 = (bf16[2048,512]{1,0:T(8,128)(2,1)S(1)}, bf16[2048,512]{1,0:T(8,128)(2,1)}, u32[]{:S(2)}) copy-start(bf16[2048,512]{1,0:T(8,128)(2,1)} %param.20) | copy-start | bytes 6291460
  132.5 6.5 %copy-start.66 = (f32[2048,1024]{1,0:T(8,128)S(1)}, f32[2048,1024]{1,0:T(8,128)}, u32[]{:S(2)}) copy-start(f32[2048,1024]{1,0:T(8,128)} %copy-done.65) | copy-start | bytes 25165828
  155.1 4.0 copy-start.6
  155.1 4.0 copy-start.12
  155.1 4.1 copy-start.19
  159.2 2.4 copy-start.64
  159.2 4.8 slice-start
  161.6 3.8 slice-start.1
  167.4 4.5 copy-start.36
  171.9 22.1 %copy-start.44 = (bf16[512,256]{0,1:T(8,128)(2,1)S(1)}, bf16[512,256]{0,1:T(8,128)(2,1)}, u32[]{:S(2)}) copy-start(bf16[512,256]{0,1:T(8,128)(2,1)} %get-tuple-element.90) | copy-start | bytes 786436
  212.4 5.4 copy-start.15
  217.7 4.5 copy-start.35
  222.2 21.9 %copy-start.42 = (bf16[512,256]{0,1:T(8,128)(2,1)S(1)}, bf16[512,256]{0,1:T(8,128)(2,1)}, u32[]{:S(2)}) copy-start(bf16[512,256]{0,1:T(8,128)(2,1)} %get-tuple-element.89) | copy-start | bytes 786436
  244.2 18.5 %copy-start.71 = (f32[4,512]{1,0:T(4,128)S(1)}, f32[4,512]{1,0:T(4,128)}, u32[]{:S(2)}) copy-start(f32[4,512]{1,0:T(4,128)} %copy-done.70) | copy-start | bytes 24580
  262.7 4.4 copy-start.14
  267.1 4.6 copy-start.34
  271.7 21.9 %copy-start.40 = (bf16[512,256]{0,1:T(8,128)(2,1)S(1)}, bf16[512,256]{0,1:T(8,128)(2,1)}, u32[]{:S(2)}) copy-start(bf16[512,256]{0,1:T(8,128)(2,1)} %get-tuple-element.87) | copy-start | bytes 786436
  293.6 18.3 %copy-start.69 = (f32[4,512]{1,0:T(4,128)S(1)}, f32[4,512]{1,0:T(4,128)}, u32[]{:S(2)}) copy-start(f32[4,512]{1,0:T(4,128)} %copy-done.68) | copy-start | bytes 24580
  311.9 4.4 copy-start.13
  316.3 4.5 copy-start.33
  320.8 21.9 %copy-start.39 = (bf16[512,256]{0,1:T(8,128)(2,1)S(1)}, bf16[512,256]{0,1:T(8,128)(2,1)}, u32[]{:S(2)}) copy-start(bf16[512,256]{0,1:T(8,128)(2,1)} %copy-done.38) | copy-start | bytes 786436
  342.7 18.6 %copy-start.22 = (f32[4,64,1024]{2,1,0:T(8,128)S(1)}, f32[4,64,1024]{2,1,0:T(8,128)}, u32[]{:S(2)}) copy-start(f32[4,64,1024]{2,1,0:T(8,128)} %fusion.44) | copy-start | bytes 3145732
  364.7 6.9 %copy-start.4 = (bf16[2048,512]{1,0:T(8,128)(2,1)S(1)}, bf16[2048,512]{1,0:T(8,128)(2,1)}, u32[]{:S(2)}) copy-start(bf16[2048,512]{1,0:T(8,128)(2,1)} %copy-done.3) | copy-start | bytes 6291460
  364.7 6.9 %copy-start.46 = (bf16[4,64,512]{2,1,0:T(8,128)(2,1)S(1)}, bf16[4,64,512]{2,1,0:T(8,128)(2,1)}, u32[]{:S(2)}) copy-start(bf16[4,64,512]{2,1,0:T(8,128)(2,1)} %fusion.110) | copy-start | bytes 786436
  364.7 6.9 %copy-start.47 = (bf16[4,64,512]{2,1,0:T(8,128)(2,1)S(1)}, bf16[4,64,512]{2,1,0:T(8,128)(2,1)}, u32[]{:S(2)}) copy-start(bf16[4,64,512]{2,1,0:T(8,128)(2,1)} %fusion.107) | copy-start | bytes 786436
  364.7 6.9 %copy-start.49 = (bf16[4,64,512]{2,1,0:T(8,128)(2,1)S(1)}, bf16[4,64,512]{2,1,0:T(8,128)(2,1)}, u32[]{:S(2)}) copy-start(bf16[4,64,512]{2,1,0:T(8,128)(2,1)} %fusion.113) | copy-start | bytes 786436
  364.7 6.9 %copy-start.51 = (bf16[4,64,512]{2,1,0:T(8,128)(2,1)S(1)}, bf16[4,64,512]{2,1,0:T(8,128)(2,1)}, u32[]{:S(2)}) copy-start(bf16[4,64,512]{2,1,0:T(8,128)(2,1)} %fusion.104) | copy-start | bytes 786436
  365.7 11.1 %collective-permute-start.3 = (bf16[256,512]{0,1:T(8,128)(2,1)S(1)}, bf16[256,512]{0,1:T(8,128)(2,1)S(1)}, u32[]{:S(2)}, u32[]{:S(2)}) collective-permute-start(bf16[256,512]{0,1:T(8,128)(2,1)S(1)} %slice.275), channel_id=1, source_target_pairs={{2,0},{4,2},{6,4},{8,6},{10,8},{12,10},{14,12},{16,14},{18,16},{20... | collective-permute-start | bytes 786440 | tf_op jit(solution)/shard_map/ppermute | solution.py:23
  367.0 15.8 %collective-permute-start.2 = (bf16[256,512]{0,1:T(8,128)(2,1)S(1)}, bf16[256,512]{0,1:T(8,128)(2,1)S(1)}, u32[]{:S(2)}, u32[]{:S(2)}) collective-permute-start(bf16[256,512]{0,1:T(8,128)(2,1)S(1)} %slice.276), channel_id=1, source_target_pairs={{0,2},{2,4},{4,6},{6,8},{8,10},{10,12},{12,14},{14,16},{16,18},{18... | collective-permute-start | bytes 786440 | tf_op jit(solution)/shard_map/ppermute | solution.py:21
  386.3 159.8 %reduce-scatter.2.cloned.1.call-start = ((), (), s32[]{:S(2)}) async-start(), calls=%async_computation.3 | async-start | bytes 3145728 | tf_op jit(solution)/shard_map/reduce_scatter | solution.py:231
  534.3 10.2 %copy-start.20 = (bf16[1024,512]{1,0:T(8,128)(2,1)S(1)}, bf16[1024,512]{1,0:T(8,128)(2,1)}, u32[]{:S(2)}) copy-start(bf16[1024,512]{1,0:T(8,128)(2,1)} %get-tuple-element.64) | copy-start | bytes 3145732
  536.2 9.9 %copy-start.54 = (f32[512]{0:T(512)S(1)}, f32[512]{0:T(512)}, u32[]{:S(2)}) copy-start(f32[512]{0:T(512)} %param.22) | copy-start | bytes 6148
  541.6 7.0 %dynamic-slice-start = ((f32[2048]{0:T(1024)}, s32[]{:T(128)}), f32[1024]{0:T(1024)S(1)}, s32[]{:S(2)}) async-start(f32[2048]{0:T(1024)} %copy-done.52, s32[]{:T(128)} %select_n.30), calls=%async_computation.5 | async-start | bytes 8704 | tf_op jit(solution)/shard_map/dynamic-slice.31
  546.1 6.9 %copy-start.1 = (bf16[512,1024]{1,0:T(8,128)(2,1)S(1)}, bf16[512,1024]{1,0:T(8,128)(2,1)}, u32[]{:S(2)}) copy-start(bf16[512,1024]{1,0:T(8,128)(2,1)} %param.28) | copy-start | bytes 3145732
  (19 other events, 32.8 us)
Sparse Core Ops, SparseCore 0:
  93.6 21.5 all-reduce.8
  132.6 22.4 all-reduce.10
  386.4 147.8 all-reduce.12
  537.0 8.6 reduce-scatter.1
where the time goes:
time: 564 us; the launch traced here: 560 us
  matrix products  287 us (51%)
  waiting for transfers between devices  191 us (34%)
  other arithmetic  45.8 us (8%)
  between operations  15 us (3%)
  starting transfers between devices  13.4 us (2%)
  local copies, waits for them, and re-layouts  7.53 us (1%)
    psum x1, waiting for transfers between devices, local(): lax.psum(grad_query_terms.astype(jnp.bfloat16), 'tm').astype(jnp.float32)  143 us
    dot_general x8, matrix products, key_grads(): jnp.einsum('hqk,qhd->khd', score_tile, query_block, preferred_element_typ...  89.7 us
    dot_general x4, matrix products, query_grads(): jnp.einsum('hqk,khd->qhd', score_tile, key_tile, preferred_element_type=j...  87.9 us
    sub x4, matrix products, softmax_rows(): weights = jnp.exp(scores - peak)  30 us
    dot_general x4, matrix products, block_context(): jnp.einsum('hqk,khd->qhd', probability.astype(jnp.bfloat16), value_block,...  22.4 us
    psum x1, waiting for transfers between devices, local(): lax.psum(partial_value.astype(jnp.bfloat16), 'ffn').astype(jnp.float32)  21.3 us
    dot_general x4, matrix products, score_grads(): jnp.einsum('qhd,khd->hqk', grad_block, value_tile, preferred_element_type...  18.2 us
    psum x1, waiting for transfers between devices, local(): lax.psum(grad_second_part.astype(jnp.bfloat16), 'ffn').astype(jnp.float32)  12.7 us
  transfers between devices with their start and end apart: 8, of which 7 were waited for; matrix products, arithmetic and copies ran while one was open for 6% of the time, Pallas kernels for 0%

commit v1 on v0

--- a/solution.py
+++ b/solution.py
@@ -8,6 +8,11 @@
 HALF = 256
 epsilon = 1e-05
 masked_score = -1e30
+
+
+def gather_and_add(x, axis):
+    parts = lax.all_gather(x, axis)
+    return jnp.sum(parts, axis=0)
 
 
 def with_halo(cells, sides, width):
@@ -238,7 +243,7 @@
     )
     weight_scale = 1.0 / math.sqrt(recording.shape[0])
     totals = (
-        lax.psum(grad_query_terms.astype(jnp.bfloat16), "tm").astype(jnp.float32),
+        gather_and_add(grad_query_terms.astype(jnp.bfloat16), "tm").astype(jnp.float32),
         lax.psum(grad_key_terms.astype(jnp.bfloat16), "tm").astype(jnp.float32),
         lax.psum(grad_value_terms.astype(jnp.bfloat16), "tm").astype(jnp.float32),
         lax.psum(grad_out_terms.astype(jnp.bfloat16), "tm").astype(jnp.float32),

time: 564 us -> 540 us (0.957)
  waiting for transfers between devices: 191 us -> 171 us
  matrix products: 287 us -> 281 us
    psum x1, waiting for transfers between devices: 143 us -> 47.9 us  [local(): lax.psum(grad_key_terms.astype(jnp.bfloat16), 'tm').astype(jnp.float32)]
    all_gather x0 -> x1, waiting for transfers between devices: none -> 73.2 us  [gather_and_add(): parts = lax.all_gather(x, axis)]
    dot_general x8, matrix products: 89.7 us -> 83.5 us  [key_grads(): jnp.einsum('hqk,qhd->khd', score_tile, query_block, preferred_element_typ...]
  transfers between devices with their start and end apart: 8 -> 9, of which waited for: 7 -> 9; matrix products, arithmetic and copies ran while one was open for 6% -> 24% of each run, Pallas kernels for 0% -> 0%
where the time goes in v1:
time: 540 us; the launch traced here: 537 us
  matrix products  281 us (52%)
  waiting for transfers between devices  171 us (32%)
  other arithmetic  47.8 us (9%)
  between operations  15 us (3%)
  starting transfers between devices  14 us (3%)
  local copies, waits for them, and re-layouts  8.24 us (2%)
    dot_general x4, matrix products, query_grads(): jnp.einsum('hqk,khd->qhd', score_tile, key_tile, preferred_element_type=j...  87.9 us
    dot_general x8, matrix products, key_grads(): jnp.einsum('hqk,qhd->khd', score_tile, query_block, preferred_element_typ...  83.5 us
    all_gather x1, waiting for transfers between devices, gather_and_add(): parts = lax.all_gather(x, axis)  73.2 us
    psum x1, waiting for transfers between devices, local(): lax.psum(grad_key_terms.astype(jnp.bfloat16), 'tm').astype(jnp.float32)  47.9 us
    sub x4, matrix products, softmax_rows(): weights = jnp.exp(scores - peak)  30 us
    dot_general x4, matrix products, block_context(): jnp.einsum('hqk,khd->qhd', probability.astype(jnp.bfloat16), value_block,...  22.3 us
    psum x1, waiting for transfers between devices, local(): lax.psum(partial_value.astype(jnp.bfloat16), 'ffn').astype(jnp.float32)  21.5 us
    dot_general x4, matrix products, score_grads(): jnp.einsum('qhd,khd->hqk', grad_block, value_tile, preferred_element_type...  18.1 us
  transfers between devices with their start and end apart: 9, of which 9 were waited for; matrix products, arithmetic and copies ran while one was open for 24% of the time, Pallas kernels for 0%

profile of v1, /device:TPU:0, one launch (start us, length us, event | category | flops | bytes accessed | tf_op | source)
XLA Modules:
  0.0 536.6 jit_solution(14578448574849368625)
XLA Ops:
  7.3 2.1 convert_reduce_fusion
  9.4 2.5 fusion.26
  11.9 2.4 fusion.24
  16.8 5.6 %collective-permute-start = (bf16[256,512]{0,1:T(8,128)(2,1)}, bf16[256,512]{0,1:T(8,128)(2,1)}, u32[]{:S(2)}, u32[]{:S(2)}) collective-permute-start(bf16[256,512]{0,1:T(8,128)(2,1)} %get-tuple-element.74), channel_id=1, source_target_pairs={{0,2},{2,4},{4,6},{6,8},{8,10},{10,12},{12,14},{14,16},{16,18},{18... | collective-permute-start | bytes 786440 | tf_op jit(solution)/shard_map/ppermute | solution.py:26
  22.4 1.8 collective-permute-start.1
  24.4 1.7 compare_and_fusion.2
  26.1 1.7 compare_and_fusion
  27.8 2.3 convolution_convert_fusion.3
  31.1 2.1 collective-permute-done
  33.2 1.9 collective-permute-done.1
  35.1 3.2 pad_maximum_fusion.5
  38.3 7.5 %fusion.168 = (f32[4,512]{1,0:T(4,128)S(1)}, f32[4,512,1024]{2,1,0:T(8,128)}) fusion(pred[512,1024]{1,0:T(8,128)(4,1)} %get-tuple-element.109, bf16[512,4,64]{0,2,1:T(8,128)(2,1)} %bitcast.161, bf16[1024,4,64]{0,2,1:T(8,128)(2,1)} %bitcast.153), kind=kOutput, calls=%fused_computation.222 | convolution fusion | flops 276825088 | bytes 9707520 | tf_op jit(solution)/shard_map/sub | solution.py:75
  45.8 5.7 %fusion.92 = bf16[4,64,512]{2,1,0:T(8,128)(2,1)} fusion(bf16[1024,4,64]{0,2,1:T(8,128)(2,1)} %bitcast.129, f32[4,512,1024]{2,1,0:T(8,128)} %get-tuple-element.105, f32[4,512]{1,0:T(4,128)S(1)} %get-tuple-element.104), kind=kOutput, calls=%fused_computation.125 | convolution fusion | flops 272760832 | bytes 9183232 | tf_op jit(solution)/shard_map/hqk,khd->qhd/dot_general | solution.py:93
  51.6 7.4 %fusion.165 = (f32[4,512]{1,0:T(4,128)S(1)}, f32[4,512,1024]{2,1,0:T(8,128)}) fusion(pred[512,1024]{1,0:T(8,128)(4,1)} %get-tuple-element.106, bf16[512,4,64]{0,2,1:T(8,128)(2,1)S(1)} %bitcast.159, bf16[1024,4,64]{0,2,1:T(8,128)(2,1)} %bitcast.151), kind=kOutput, calls=%fused_computation.219 | convolution fusion | flops 276825088 | bytes 9707520 | tf_op jit(solution)/shard_map/sub | solution.py:75
  59.0 5.8 %fusion.101 = bf16[4,64,512]{2,1,0:T(8,128)(2,1)} fusion(bf16[1024,4,64]{0,2,1:T(8,128)(2,1)} %bitcast.127, f32[4,512,1024]{2,1,0:T(8,128)} %get-tuple-element.99, f32[4,512]{1,0:T(4,128)S(1)} %get-tuple-element.98), kind=kOutput, calls=%fused_computation.128 | convolution fusion | flops 272760832 | bytes 9183232 | tf_op jit(solution)/shard_map/hqk,khd->qhd/dot_general | solution.py:93
  64.7 7.6 %fusion.166 = (f32[4,512]{1,0:T(4,128)S(1)}, f32[4,512,1024]{2,1,0:T(8,128)}) fusion(pred[512,1024]{1,0:T(8,128)(4,1)} %get-tuple-element.107, bf16[512,4,64]{0,2,1:T(8,128)(2,1)S(1)} %bitcast.163, bf16[1024,4,64]{0,2,1:T(8,128)(2,1)} %bitcast.155), kind=kOutput, calls=%fused_computation.220 | convolution fusion | flops 276825088 | bytes 9707520 | tf_op jit(solution)/shard_map/sub | solution.py:75
  72.3 5.7 %fusion.98 = bf16[4,64,512]{2,1,0:T(8,128)(2,1)} fusion(bf16[1024,4,64]{0,2,1:T(8,128)(2,1)} %bitcast.131, f32[4,512,1024]{2,1,0:T(8,128)} %get-tuple-element.101, f32[4,512]{1,0:T(4,128)S(1)} %get-tuple-element.100), kind=kOutput, calls=%fused_computation.127 | convolution fusion | flops 272760832 | bytes 9183232 | tf_op jit(solution)/shard_map/hqk,khd->qhd/dot_general | solution.py:93
  78.1 7.5 %fusion.167 = (f32[4,512]{1,0:T(4,128)S(1)}, f32[4,512,1024]{2,1,0:T(8,128)}) fusion(pred[512,1024]{1,0:T(8,128)(4,1)} %get-tuple-element.108, bf16[512,4,64]{0,2,1:T(8,128)(2,1)} %bitcast.165, bf16[1024,4,64]{0,2,1:T(8,128)(2,1)} %bitcast.157), kind=kOutput, calls=%fused_computation.221 | convolution fusion | flops 276825088 | bytes 9707520 | tf_op jit(solution)/shard_map/sub | solution.py:75
  85.6 5.1 fusion.95
  91.4 2.1 convolution_convert_fusion.1
  93.7 21.5 %all-reduce.9.cloned.1.call-done = bf16[2048,512]{1,0:T(8,128)(2,1)} async-done(((bf16[2048,512]{1,0:T(8,128)(2,1)}), bf16[2048,512]{1,0:T(8,128)(2,1)}) %all-reduce.9.cloned.1.call-update) | async-done | bytes 2097168 | tf_op jit(solution)/shard_map/psum | solution.py:169
  115.2 2.4 fusion.68
  118.6 2.8 fusion.162
  121.4 5.3 multiply_convert_fusion.5
  126.7 1.9 copy-done.64
  128.7 3.8 convolution_convert_fusion
  132.5 6.5 %convolution_convert_fusion.6 = bf16[512,1024]{1,0:T(8,128)(2,1)} fusion(bf16[2048,1024]{1,0:T(8,128)(2,1)} %copy-done.64, bf16[2048,512]{1,0:T(8,128)(2,1)} %all-reduce.9.cloned.1.call-done, bf16[2048,512]{1,0:T(8,128)(2,1)S(1)} %copy-done.2, f32[512]{0:T(512)S(1)} %copy-done.52, f32[2048]{0:T(1024)S(1)} %add_rsqrt_fusion, ...), kind=kOutput, calls=%fused_computation.124 | convolution fusion | flops 2155347968 | bytes 9455616 | tf_op jit(solution)/shard_map/dot_general | solution.py:180
  139.0 3.4 multiply_convert_fusion.9
  142.4 12.7 %all-reduce.11.cloned.1.call-done = bf16[2048,512]{1,0:T(8,128)(2,1)} async-done(((bf16[2048,512]{1,0:T(8,128)(2,1)}), bf16[2048,512]{1,0:T(8,128)(2,1)}) %all-reduce.11.cloned.1.call-update) | async-done | bytes 2097168 | tf_op jit(solution)/shard_map/psum | solution.py:182
  155.1 4.1 fusion.29
  159.2 2.3 multiply_add_fusion
  162.5 1.9 fusion.81
  165.5 4.5 fusion.170
  170.1 1.9 fusion.77
  172.0 4.5 fusion.171
  177.8 4.5 fusion.169
  183.5 4.5 fusion.172
  188.1 18.3 %fusion.50 = f32[4,64,1024]{2,1,0:T(8,128)} fusion(bf16[512,4,64]{0,2,1:T(8,128)(2,1)S(1)} %bitcast.166, f32[4,512,1024]{2,1,0:T(8,128)} %fusion.170, f32[4,512,1024]{2,1,0:T(8,128)} %get-tuple-element.103, f32[4,512]{1,0:T(4,128)S(1)} %get-tuple-element.102), kind=kOutput, calls=%fused_computation.73 | convolution fusion | flops 283118592 | bytes 18096128 | tf_op jit(solution)/shard_map/hqk,qhd->khd/dot_general | solution.py:88
  206.3 18.5 %fusion.56 = f32[4,64,1024]{2,1,0:T(8,128)} fusion(bf16[512,4,64]{0,2,1:T(8,128)(2,1)S(1)} %bitcast.164, f32[4,512,1024]{2,1,0:T(8,128)} %fusion.171, f32[4,512,1024]{2,1,0:T(8,128)} %get-tuple-element.101, f32[4,512]{1,0:T(4,128)S(1)} %get-tuple-element.100), kind=kOutput, calls=%fused_computation.75 | convolution fusion | flops 283118592 | bytes 18096128 | tf_op jit(solution)/shard_map/hqk,qhd->khd/dot_general | solution.py:88
  224.8 22.2 %fusion.44 = f32[4,64,1024]{2,1,0:T(8,128)S(1)} fusion(bf16[512,4,64]{0,2,1:T(8,128)(2,1)} %bitcast.162, f32[4,512,1024]{2,1,0:T(8,128)} %fusion.169, f32[4,512,1024]{2,1,0:T(8,128)} %get-tuple-element.105, f32[4,512]{1,0:T(4,128)S(1)} %get-tuple-element.104), kind=kOutput, calls=%fused_computation.71 | convolution fusion | flops 283118592 | bytes 18096128 | tf_op jit(solution)/shard_map/hqk,qhd->khd/dot_general | solution.py:88
  247.0 18.3 %fusion.62 = f32[4,64,1024]{2,1,0:T(8,128)} fusion(bf16[512,4,64]{0,2,1:T(8,128)(2,1)S(1)} %bitcast.160, f32[4,512,1024]{2,1,0:T(8,128)} %fusion.172, f32[4,512,1024]{2,1,0:T(8,128)} %get-tuple-element.99, f32[4,512]{1,0:T(4,128)S(1)} %get-tuple-element.98), kind=kOutput, calls=%fused_computation.77 | convolution fusion | flops 283118592 | bytes 18096128 | tf_op jit(solution)/shard_map/hqk,qhd->khd/dot_general | solution.py:88
  271.2 4.6 collective-permute-start.2
  277.2 3.7 collective-permute-done.3
  280.9 6.0 %collective-permute-done.2 = bf16[256,512]{0,1:T(8,128)(2,1)S(1)} collective-permute-done((bf16[256,512]{0,1:T(8,128)(2,1)S(1)}, bf16[256,512]{0,1:T(8,128)(2,1)S(1)}, u32[]{:S(2)}, u32[]{:S(2)}) %collective-permute-start.2) | collective-permute-done | bytes 262176 | tf_op jit(solution)/shard_map/ppermute | solution.py:26
  288.6 1.5 convolution_convert_fusion.9
  290.1 1.5 convolution_convert_fusion.8
  291.6 21.7 %fusion.110 = bf16[4,64,512]{2,1,0:T(8,128)(2,1)S(1)} fusion(bf16[1024,4,64]{0,2,1:T(8,128)(2,1)S(1)} %bitcast.158, f32[4,512,1024]{2,1,0:T(8,128)} %fusion.170, f32[4,512,1024]{2,1,0:T(8,128)} %get-tuple-element.103, f32[4,512]{1,0:T(4,128)S(1)} %get-tuple-element.102), kind=kOutput, calls=%fused_computation.131 | convolution fusion | flops 283249664 | bytes 17571840 | tf_op jit(solution)/shard_map/hqk,khd->qhd/dot_general | solution.py:84
  313.4 22.1 %fusion.107 = bf16[4,64,512]{2,1,0:T(8,128)(2,1)} fusion(bf16[1024,4,64]{0,2,1:T(8,128)(2,1)S(1)} %bitcast.156, f32[4,512,1024]{2,1,0:T(8,128)} %fusion.171, f32[4,512,1024]{2,1,0:T(8,128)} %get-tuple-element.101, f32[4,512]{1,0:T(4,128)S(1)} %get-tuple-element.100), kind=kOutput, calls=%fused_computation.130 | convolution fusion | flops 283249664 | bytes 17571840 | tf_op jit(solution)/shard_map/hqk,khd->qhd/dot_general | solution.py:84
  335.5 22.1 %fusion.113 = bf16[4,64,512]{2,1,0:T(8,128)(2,1)} fusion(bf16[1024,4,64]{0,2,1:T(8,128)(2,1)S(1)} %bitcast.154, f32[4,512,1024]{2,1,0:T(8,128)} %fusion.169, f32[4,512,1024]{2,1,0:T(8,128)} %get-tuple-element.105, f32[4,512]{1,0:T(4,128)S(1)} %get-tuple-element.104), kind=kOutput, calls=%fused_computation.132 | convolution fusion | flops 283249664 | bytes 17571840 | tf_op jit(solution)/shard_map/hqk,khd->qhd/dot_general | solution.py:84
  357.6 22.0 %fusion.104 = bf16[4,64,512]{2,1,0:T(8,128)(2,1)} fusion(bf16[1024,4,64]{0,2,1:T(8,128)(2,1)S(1)} %bitcast.152, f32[4,512,1024]{2,1,0:T(8,128)} %fusion.172, f32[4,512,1024]{2,1,0:T(8,128)} %get-tuple-element.99, f32[4,512]{1,0:T(4,128)S(1)} %get-tuple-element.98), kind=kOutput, calls=%fused_computation.129 | convolution fusion | flops 283249664 | bytes 17571840 | tf_op jit(solution)/shard_map/hqk,khd->qhd/dot_general | solution.py:84
  379.6 2.0 fusion.132
  382.6 2.1 add_convert_fusion
  385.0 1.5 convolution_convert_fusion.10
  386.5 47.9 %all-reduce.13.cloned.1.call-done = (bf16[512,256]{1,0:T(8,128)(2,1)}, bf16[512,256]{1,0:T(8,128)(2,1)}, bf16[256,512]{1,0:T(8,128)(2,1)}, bf16[512,1024]{1,0:T(8,128)(2,1)}, bf16[1024,512]{1,0:T(8,128)(2,1)}) async-done(((bf16[512,256]{1,0:T(8,128)(2,1)}, bf16[512,256]{1,0:T(8,128)(2,1)}, bf16[256,512]{1,0:T(8,128)(2,1)}, bf16[512,1024]{1,0:T(8,128)(2,1)}, bf16[1024,512]{1,0:T(8,128)(2,1)}), ...) | async-done | bytes 2883600 | tf_op jit(solution)/shard_map/psum | solution.py:247
  434.4 1.9 convert_multiply_fusion.6
  436.3 1.8 convert_multiply_fusion.5
  438.1 1.8 convert_multiply_fusion.4
  439.9 2.8 convert_multiply_fusion.2
  442.7 1.6 convert_multiply_fusion.1
  444.4 1.6 reduce-scatter.2.cloned.1.call-done
  446.0 2.4 fusion.72
  448.4 4.5 multiply_add_fusion.1
  452.9 73.2 %all-gather.3.cloned.1.call-done = bf16[8192,256]{1,0:T(8,128)(2,1)} async-done(((bf16[512,256]{1,0:T(8,128)(2,1)}), bf16[8192,256]{1,0:T(8,128)(2,1)}) %all-gather.3.cloned.1.call-update) | async-done | bytes 4194320 | tf_op jit(solution)/shard_map/all_gather | solution.py:14
  526.1 2.9 reduce_sum.188
  (192 shorter events, 21.2 us)
Async XLA Ops:
  7.2 111.4 %copy-start = (bf16[512,1024]{1,0:T(8,128)(2,1)S(1)}, bf16[512,1024]{1,0:T(8,128)(2,1)}, u32[]{:S(2)}) copy-start(bf16[512,1024]{1,0:T(8,128)(2,1)} %param.28) | copy-start | bytes 3145732
  7.2 4.7 copy-start.2
  7.2 4.7 copy-start.50
  7.2 108.0 %all-reduce.9.cloned.1.call-start = ((), (), s32[]{:S(2)}) async-start(), calls=%async_computation.1 | async-start | bytes 4194304 | tf_op jit(solution)/shard_map/psum | solution.py:169
  11.9 2.5 copy-start.49
  11.9 2.5 copy-start.31
  11.9 3.2 copy-start.29
  14.3 2.5 copy-start.3
  14.3 9.9 %copy-start.39 = (s32[32768]{0:T(1024)S(1)}, s32[32768]{0:T(1024)}, u32[]{:S(2)}) copy-start(s32[32768]{0:T(1024)} %param.21) | copy-start | bytes 393220
  15.1 12.7 %copy-start.33 = (bf16[512,256]{1,0:T(8,128)(2,1)S(1)}, bf16[512,256]{1,0:T(8,128)(2,1)}, u32[]{:S(2)}) copy-start(bf16[512,256]{1,0:T(8,128)(2,1)} %param.23) | copy-start | bytes 786436
  15.9 6.5 %copy-start.11 = (bf16[2048,256]{0,1:T(8,128)(2,1)}, bf16[2048,256]{0,1:T(8,128)(2,1)S(1)}, u32[]{:S(2)}) copy-start(bf16[2048,256]{0,1:T(8,128)(2,1)S(1)} %convolution_convert_fusion.5) | copy-start | bytes 3145732
  16.8 16.4 %collective-permute-start = (bf16[256,512]{0,1:T(8,128)(2,1)}, bf16[256,512]{0,1:T(8,128)(2,1)}, u32[]{:S(2)}, u32[]{:S(2)}) collective-permute-start(bf16[256,512]{0,1:T(8,128)(2,1)} %get-tuple-element.74), channel_id=1, source_target_pairs={{0,2},{2,4},{4,6},{6,8},{8,10},{10,12},{12,14},{14,16},{16,18},{18... | collective-permute-start | bytes 786440 | tf_op jit(solution)/shard_map/ppermute | solution.py:26
  22.4 12.7 %collective-permute-start.1 = (bf16[256,512]{0,1:T(8,128)(2,1)}, bf16[256,512]{0,1:T(8,128)(2,1)}, u32[]{:S(2)}, u32[]{:S(2)}) collective-permute-start(bf16[256,512]{0,1:T(8,128)(2,1)} %get-tuple-element.75), channel_id=1, source_target_pairs={{2,0},{4,2},{6,4},{8,6},{10,8},{12,10},{14,12},{16,14},{18,16},{20... | collective-permute-start | bytes 786440 | tf_op jit(solution)/shard_map/ppermute | solution.py:28
  24.2 10.9 %copy-start.10 = (bf16[2048,256]{0,1:T(8,128)(2,1)S(1)}, bf16[2048,256]{0,1:T(8,128)(2,1)}, u32[]{:S(2)}) copy-start(bf16[2048,256]{0,1:T(8,128)(2,1)} %copy-done.9) | copy-start | bytes 3145732
  24.2 10.9 %copy-start.12 = (bf16[2048,256]{0,1:T(8,128)(2,1)S(1)}, bf16[2048,256]{0,1:T(8,128)(2,1)}, u32[]{:S(2)}) copy-start(bf16[2048,256]{0,1:T(8,128)(2,1)} %copy-done.11) | copy-start | bytes 3145732
  31.1 20.5 %copy-start.40 = (bf16[512,256]{0,1:T(8,128)(2,1)}, bf16[512,256]{0,1:T(8,128)(2,1)S(1)}, u32[]{:S(2)}) copy-start(bf16[512,256]{0,1:T(8,128)(2,1)S(1)} %get-tuple-element.87) | copy-start | bytes 786436
  59.0 5.8 %copy-start.42 = (bf16[512,256]{0,1:T(8,128)(2,1)S(1)}, bf16[512,256]{0,1:T(8,128)(2,1)}, u32[]{:S(2)}) copy-start(bf16[512,256]{0,1:T(8,128)(2,1)} %get-tuple-element.88) | copy-start | bytes 786436
  85.5 5.8 %copy-start.44 = (bf16[256,512]{1,0:T(8,128)(2,1)S(1)}, bf16[256,512]{1,0:T(8,128)(2,1)}, u32[]{:S(2)}) copy-start(bf16[256,512]{1,0:T(8,128)(2,1)} %param.26) | copy-start | bytes 786436
  85.5 5.8 %copy-start.54 = (bf16[4,64,512]{2,1,0:T(8,128)(2,1)S(1)}, bf16[4,64,512]{2,1,0:T(8,128)(2,1)}, u32[]{:S(2)}) copy-start(bf16[4,64,512]{2,1,0:T(8,128)(2,1)} %fusion.92) | copy-start | bytes 786436
  85.5 5.8 %copy-start.56 = (bf16[4,64,512]{2,1,0:T(8,128)(2,1)S(1)}, bf16[4,64,512]{2,1,0:T(8,128)(2,1)}, u32[]{:S(2)}) copy-start(bf16[4,64,512]{2,1,0:T(8,128)(2,1)} %fusion.101) | copy-start | bytes 786436
  85.6 5.8 %copy-start.58 = (bf16[4,64,512]{2,1,0:T(8,128)(2,1)S(1)}, bf16[4,64,512]{2,1,0:T(8,128)(2,1)}, u32[]{:S(2)}) copy-start(bf16[4,64,512]{2,1,0:T(8,128)(2,1)} %fusion.98) | copy-start | bytes 786436
  93.5 25.1 %copy-start.52 = (f32[512]{0:T(512)S(1)}, f32[512]{0:T(512)}, u32[]{:S(2)}) copy-start(f32[512]{0:T(512)} %param.27) | copy-start | bytes 6148
  93.5 61.6 %all-reduce.11.cloned.1.call-start = ((), (), s32[]{:S(2)}) async-start(), calls=%async_computation.2 | async-start | bytes 4194304 | tf_op jit(solution)/shard_map/psum | solution.py:182
  118.6 2.8 copy-start.20
  118.6 2.8 copy-start.53
  121.4 5.3 copy-start.62
  132.5 302.0 %all-reduce.13.cloned.1.call-start = ((), (), s32[]{:S(2)}) async-start(), calls=%async_computation.5 | async-start | bytes 5767168 | tf_op jit(solution)/shard_map/psum | solution.py:247
  132.5 6.5 %copy-start.21 = (bf16[2048,512]{1,0:T(8,128)(2,1)S(1)}, bf16[2048,512]{1,0:T(8,128)(2,1)}, u32[]{:S(2)}) copy-start(bf16[2048,512]{1,0:T(8,128)(2,1)} %param.20) | copy-start | bytes 6291460
  132.5 6.5 %copy-start.63 = (f32[2048,1024]{1,0:T(8,128)S(1)}, f32[2048,1024]{1,0:T(8,128)}, u32[]{:S(2)}) copy-start(f32[2048,1024]{1,0:T(8,128)} %copy-done.62) | copy-start | bytes 25165828
  155.1 4.1 copy-start.6
  155.1 4.1 copy-start.15
  155.1 4.1 copy-start.22
  155.1 7.4 %slice-start.6 = ((s8[8388608]{0:T(1024)(128)(4,1)}), s8[4194304]{0:T(1024)(128)(4,1)S(1)}, s32[]{:S(2)}) async-start(s8[8388608]{0:T(1024)(128)(4,1)} %bitcast.189), calls=%async_computation.13 | async-start | bytes 8388608
  159.2 3.2 slice-start.7
  161.6 2.8 copy-start.7
  161.6 8.5 %slice-start.4 = ((s8[8388608]{0:T(1024)(128)(4,1)}), s8[4194304]{0:T(1024)(128)(4,1)S(1)}, s32[]{:S(2)}) async-start(s8[8388608]{0:T(1024)(128)(4,1)} %bitcast.187), calls=%async_computation.11 | async-start | bytes 8388608
  162.5 3.0 copy-start.19
  162.5 7.6 %slice-start.5 = ((s8[8388608]{0:T(1024)(128)(4,1)}), s8[4194304]{0:T(1024)(128)(4,1)S(1)}, s32[]{:S(2)}) async-start(s8[8388608]{0:T(1024)(128)(4,1)} %bitcast.187), calls=%async_computation.12 | async-start | bytes 8388608
  165.5 11.0 %slice-start = ((s8[8388608]{0:T(1024)(128)(4,1)}), s8[4194304]{0:T(1024)(128)(4,1)S(1)}, s32[]{:S(2)}) async-start(s8[8388608]{0:T(1024)(128)(4,1)} %bitcast.183), calls=%async_computation.7 | async-start | bytes 8388608
  170.1 6.5 %slice-start.1 = ((s8[8388608]{0:T(1024)(128)(4,1)}), s8[4194304]{0:T(1024)(128)(4,1)S(1)}, s32[]{:S(2)}) async-start(s8[8388608]{0:T(1024)(128)(4,1)} %bitcast.183), calls=%async_computation.8 | async-start | bytes 8388608
  172.0 10.3 %slice-start.2 = ((s8[8388608]{0:T(1024)(128)(4,1)}), s8[4194304]{0:T(1024)(128)(4,1)S(1)}, s32[]{:S(2)}) async-start(s8[8388608]{0:T(1024)(128)(4,1)} %bitcast.185), calls=%async_computation.9 | async-start | bytes 8388608
  176.6 5.7 %slice-start.3 = ((s8[8388608]{0:T(1024)(128)(4,1)}), s8[4194304]{0:T(1024)(128)(4,1)S(1)}, s32[]{:S(2)}) async-start(s8[8388608]{0:T(1024)(128)(4,1)} %bitcast.185), calls=%async_computation.10 | async-start | bytes 8388608
  183.5 4.6 copy-start.43
  224.8 22.2 %copy-start.41 = (bf16[512,256]{0,1:T(8,128)(2,1)S(1)}, bf16[512,256]{0,1:T(8,128)(2,1)}, u32[]{:S(2)}) copy-start(bf16[512,256]{0,1:T(8,128)(2,1)} %copy-done.40) | copy-start | bytes 786436
  268.7 7.0 %copy-start.8 = (f32[2048,512]{1,0:T(8,128)S(1)}, f32[2048,512]{1,0:T(8,128)}, u32[]{:S(2)}) copy-start(f32[2048,512]{1,0:T(8,128)} %copy-done.7) | copy-start | bytes 12582916
  268.7 7.0 %copy-start.55 = (bf16[4,64,512]{2,1,0:T(8,128)(2,1)S(1)}, bf16[4,64,512]{2,1,0:T(8,128)(2,1)}, u32[]{:S(2)}) copy-start(bf16[4,64,512]{2,1,0:T(8,128)(2,1)} %fusion.92) | copy-start | bytes 786436
  268.7 7.0 %copy-start.57 = (bf16[4,64,512]{2,1,0:T(8,128)(2,1)S(1)}, bf16[4,64,512]{2,1,0:T(8,128)(2,1)}, u32[]{:S(2)}) copy-start(bf16[4,64,512]{2,1,0:T(8,128)(2,1)} %fusion.101) | copy-start | bytes 786436
  268.7 7.0 %copy-start.59 = (bf16[4,64,512]{2,1,0:T(8,128)(2,1)S(1)}, bf16[4,64,512]{2,1,0:T(8,128)(2,1)}, u32[]{:S(2)}) copy-start(bf16[4,64,512]{2,1,0:T(8,128)(2,1)} %fusion.98) | copy-start | bytes 786436
  268.7 7.0 %copy-start.61 = (bf16[4,64,512]{2,1,0:T(8,128)(2,1)S(1)}, bf16[4,64,512]{2,1,0:T(8,128)(2,1)}, u32[]{:S(2)}) copy-start(bf16[4,64,512]{2,1,0:T(8,128)(2,1)} %copy-done.60) | copy-start | bytes 786436
  269.7 11.2 %collective-permute-start.3 = (bf16[256,512]{0,1:T(8,128)(2,1)S(1)}, bf16[256,512]{0,1:T(8,128)(2,1)S(1)}, u32[]{:S(2)}, u32[]{:S(2)}) collective-permute-start(bf16[256,512]{0,1:T(8,128)(2,1)S(1)} %slice.275), channel_id=1, source_target_pairs={{2,0},{4,2},{6,4},{8,6},{10,8},{12,10},{14,12},{16,14},{18,16},{20... | collective-permute-start | bytes 786440 | tf_op jit(solution)/shard_map/ppermute | solution.py:28
  271.2 15.8 %collective-permute-start.2 = (bf16[256,512]{0,1:T(8,128)(2,1)S(1)}, bf16[256,512]{0,1:T(8,128)(2,1)S(1)}, u32[]{:S(2)}, u32[]{:S(2)}) collective-permute-start(bf16[256,512]{0,1:T(8,128)(2,1)S(1)} %slice.276), channel_id=1, source_target_pairs={{0,2},{2,4},{4,6},{6,8},{8,10},{10,12},{12,14},{14,16},{16,18},{18... | collective-permute-start | bytes 786440 | tf_op jit(solution)/shard_map/ppermute | solution.py:26
  291.6 21.8 %copy-start.37 = (bf16[1024,256]{0,1:T(8,128)(2,1)S(1)}, bf16[1024,256]{0,1:T(8,128)(2,1)}, u32[]{:S(2)}) copy-start(bf16[1024,256]{0,1:T(8,128)(2,1)} %get-tuple-element.82) | copy-start | bytes 1572868
  291.6 154.4 %reduce-scatter.2.cloned.1.call-start = ((), (), s32[]{:S(2)}) async-start(), calls=%async_computation.3 | async-start | bytes 3145728 | tf_op jit(solution)/shard_map/reduce_scatter | solution.py:236
  313.3 22.1 %copy-start.36 = (bf16[1024,256]{0,1:T(8,128)(2,1)S(1)}, bf16[1024,256]{0,1:T(8,128)(2,1)}, u32[]{:S(2)}) copy-start(bf16[1024,256]{0,1:T(8,128)(2,1)} %get-tuple-element.66) | copy-start | bytes 1572868
  335.5 22.1 %copy-start.35 = (bf16[1024,256]{0,1:T(8,128)(2,1)S(1)}, bf16[1024,256]{0,1:T(8,128)(2,1)}, u32[]{:S(2)}) copy-start(bf16[1024,256]{0,1:T(8,128)(2,1)} %get-tuple-element.72) | copy-start | bytes 1572868
  357.6 22.0 %copy-start.34 = (bf16[512,256]{1,0:T(8,128)(2,1)S(1)}, bf16[512,256]{1,0:T(8,128)(2,1)}, u32[]{:S(2)}) copy-start(bf16[512,256]{1,0:T(8,128)(2,1)} %param.23) | copy-start | bytes 786436
  382.6 2.4 copy-start.46
  382.6 2.4 copy-start.47
  382.6 2.4 copy-start.48
  384.7 141.4 %all-gather.3.cloned.1.call-start = ((), (), s32[]{:S(2)}) async-start(), calls=%async_computation.4 | async-start | bytes 4456448 | tf_op jit(solution)/shard_map/all_gather | solution.py:14
  434.4 8.3 %copy-start.23 = (bf16[1024,512]{1,0:T(8,128)(2,1)S(1)}, bf16[1024,512]{1,0:T(8,128)(2,1)}, u32[]{:S(2)}) copy-start(bf16[1024,512]{1,0:T(8,128)(2,1)} %get-tuple-element.63) | copy-start | bytes 3145732
  434.4 11.5 %copy-start.51 = (f32[512]{0:T(512)S(1)}, f32[512]{0:T(512)}, u32[]{:S(2)}) copy-start(f32[512]{0:T(512)} %param.22) | copy-start | bytes 6148
  439.9 8.5 %dynamic-slice-start = ((f32[2048]{0:T(1024)}, s32[]{:T(128)}), f32[1024]{0:T(1024)S(1)}, s32[]{:S(2)}) async-start(f32[2048]{0:T(1024)} %copy-done.49, s32[]{:T(128)} %select_n.30), calls=%async_computation.6 | async-start | bytes 8704 | tf_op jit(solution)/shard_map/dynamic-slice.31
  448.4 81.4 %copy-start.1 = (bf16[512,1024]{1,0:T(8,128)(2,1)S(1)}, bf16[512,1024]{1,0:T(8,128)(2,1)}, u32[]{:S(2)}) copy-start(bf16[512,1024]{1,0:T(8,128)(2,1)} %param.28) | copy-start | bytes 3145732
  (19 other events, 30.4 us)
Sparse Core Ops, SparseCore 0:
  93.6 21.5 all-reduce.8
  132.6 22.4 all-reduce.10
  291.7 142.6 all-reduce.12
  437.1 8.8 reduce-scatter.1
  449.2 76.8 all-gather.2
